TPU v7x, 32 devices: a whole 2x2x4 slice. The times are simulated.
32 devices in a mesh: rep: 2 (over y), ep: 8 (over z, x), tp: 2 (over core).
Axes of the slice: x: 2, y: 2, z: 4, core: 2. Of those that a mesh axis runs over, the one named last changes fastest.
Arguments:
- tokens: bfloat16 [2048, 3584], P(('rep', 'ep'), 'tp'), parts along dimension 0, may hold values from -6 to 6
- expert_ids: int32 [2048, 8], P(('rep', 'ep')), parts along dimension 0, may hold values from 0 to 63, all different within a row; in each aligned block of 512 rows (0 to 511, 512 to 1023, ...) at most 128 rows name the same one
- gate_values: float32 [2048, 8], P(('rep', 'ep')), parts along dimension 0, may hold values from 0.1 to 1
- group_counts: int32 [4], P('rep'), parts along dimension 0, may hold values from 256 to 512
- gate_weight: bfloat16 [14336, 2560], P(('rep', 'ep'), 'tp'), parts along dimension 0, may hold values from -0.09375 to 0.09375
- up_weight: bfloat16 [14336, 2560], P(('rep', 'ep'), 'tp'), parts along dimension 0, may hold values from -0.09375 to 0.09375
- down_weight: bfloat16 [14336, 2560], P(('rep', 'ep'), 'tp'), parts along dimension 0, may hold values from -0.125 to 0.125
Outputs:
- expert_output: bfloat16 [2048, 3584], P(('rep', 'ep'), 'tp'), parts along dimension 0
There are 2 independent parts, one for each index of `rep`. A program takes and returns all parts, laid end to end along the dimension named above; each array names one. Nothing has to cross between parts.
Inputs may be any that keep to these rules, and one draw needn't show every extreme that they name: `expert_ids`: each row names 8 different experts; within the 512 rows of one rollout group no expert is named by more than 128 rows.
All inputs are finite; a program needn't handle non-finite values.
Results may differ from a plain program's by a relative error of at most 0.014.
Values may be sent and summed in bfloat16 or wider, within the bound.
A program may use at most 128 MiB of HBM per device.

v0:
```python
import jax
import jax.numpy as jnp
from jax import lax
from jax.sharding import PartitionSpec as P

D = 3584
FF = 2560
WAVE = 2
MEMBERS = 8
GROUP_EP = 4
TOK_G = 512
CAP = 128


def as_sent(array):

    def short(part):
        return part.astype(jnp.bfloat16) if part.dtype == jnp.float32 else part

    return jax.tree.map(short, array)


def swapped(array, axis, distance):
    return lax.ppermute(array, axis, [(i, i ^ 1 << distance) for i in range(lax.axis_size(axis))])


def dispatch_slots(expert_ids, gate_values, live_count, expert):
    row_index = jnp.arange(TOK_G, dtype=jnp.int32)
    live_rows = row_index < live_count
    hit_mask = expert_ids == expert
    selected = jnp.logical_and(jnp.any(hit_mask, axis=1), live_rows)
    row_weight = jnp.sum(jnp.where(hit_mask, gate_values, jnp.float32(0.0)), axis=1)
    position = jnp.cumsum(selected.astype(jnp.int32)) - 1
    slot_index = jnp.arange(CAP, dtype=jnp.int32)
    slot_match = jnp.logical_and(position[None, :] == slot_index[:, None], selected[None, :])
    slot_rows = jnp.sum(jnp.where(slot_match, row_index[None, :], 0), axis=1)
    slot_valid = jnp.any(slot_match, axis=1)
    slot_weight = jnp.where(slot_valid, row_weight[slot_rows], jnp.float32(0.0))
    return (slot_rows, slot_weight)


def shards(tokens, expert_ids, gate_values, group_counts, gate_weight, up_weight, down_weight):
    ep_index = lax.axis_index("ep")
    slice_width = FF // MEMBERS
    group_bits = GROUP_EP.bit_length() - 1
    weight_stack = jnp.stack([gate_weight, up_weight, down_weight])
    rows_held = weight_stack.shape[1]
    pieces = weight_stack.shape[2] // slice_width
    slice_blocks = weight_stack.reshape(3, rows_held, pieces, slice_width).transpose(0, 2, 1, 3)
    fan_out = lax.axis_size("ep") // pieces
    outgoing = jnp.tile(slice_blocks, (1, fan_out, 1, 1))
    arrived = lax.all_to_all(outgoing, "ep", split_axis=1, concat_axis=1, tiled=True)
    columns = arrived.reshape(3, -1, slice_width)
    features = lax.all_gather(tokens, "tp", axis=1, tiled=True)
    group_data = (features, expert_ids, gate_values)
    for bit_level in range(group_bits):
        received = jax.tree.map(
            lambda part, own: part.astype(own.dtype),
            swapped(as_sent(group_data), "ep", bit_level),
            group_data,
        )
        upper_half = ep_index >> bit_level & 1 == 1
        group_data = tuple(
            (
                jnp.where(
                    upper_half, jnp.concatenate([other, own], 0), jnp.concatenate([own, other], 0)
                )
                for own, other in zip(group_data, received)
            )
        )
    group_tokens, group_ids, group_gates = group_data
    live_count = lax.dynamic_index_in_dim(group_counts, ep_index // GROUP_EP, keepdims=False)
    partials = jnp.zeros((group_tokens.shape[0], D), jnp.float32)
    for expert in range(WAVE):
        slot_rows, slot_weight = dispatch_slots(group_ids, group_gates, live_count, expert)
        expert_rows = group_tokens[slot_rows]
        gate_cols = columns[0, expert * D : (expert + 1) * D]
        up_cols = columns[1, expert * D : (expert + 1) * D]
        down_cols = columns[2, expert * D : (expert + 1) * D]
        gate_act = jnp.dot(expert_rows, gate_cols, preferred_element_type=jnp.float32)
        up_act = jnp.dot(expert_rows, up_cols, preferred_element_type=jnp.float32)
        hidden = (jax.nn.silu(gate_act) * up_act).astype(jnp.bfloat16)
        projected = lax.dot_general(
            hidden, down_cols, (((1,), (1,)), ((), ())), preferred_element_type=jnp.float32
        )
        partials = partials.at[slot_rows].add(slot_weight[:, None] * projected)
    rounded = lax.optimization_barrier(partials.astype(jnp.bfloat16)).astype(jnp.float32)
    halved = lax.psum_scatter(
        rounded.astype(jnp.bfloat16), "tp", scatter_dimension=1, tiled=True
    ).astype(jnp.float32)
    for bit_level in reversed(range(group_bits)):
        paired_up = halved.reshape(2, -1, halved.shape[1])
        upper_half = ep_index >> bit_level & 1 == 1
        kept_part = jnp.where(upper_half, paired_up[1], paired_up[0])
        sent_part = jnp.where(upper_half, paired_up[0], paired_up[1])
        halved = kept_part + swapped(sent_part.astype(jnp.bfloat16), "ep", bit_level).astype(
            sent_part.dtype
        )
    return halved.astype(jnp.bfloat16)


def solution(mesh):
    placed = (
        P(("rep", "ep"), "tp"),
        P(("rep", "ep"), None),
        P(("rep", "ep"), None),
        P("rep"),
        P(("rep", "ep"), "tp"),
        P(("rep", "ep"), "tp"),
        P(("rep", "ep"), "tp"),
    )
    return jax.shard_map(
        shards, mesh=mesh, in_specs=placed, out_specs=P(("rep", "ep"), "tp"), check_vma=False
    )
```

profile of v0, /device:TPU:0, one launch (start us, length us, event | category | flops | bytes accessed | tf_op | source)
XLA Modules:
  0.0 490.2 jit_solution(13979676332622343331)
XLA Ops:
  6.5 4.6 copy.24
  11.1 3.2 copy.23
  14.3 4.3 copy.22
  18.7 3.9 maximum_bitcast_fusion
  23.2 7.2 %tile.4 = bf16[3,2,4,896,320]{3,4,0,2,1:T(8,128)(2,1)} broadcast(bf16[3,4,896,320]{2,3,0,1:T(8,128)(2,1)S(1)} %copy.25), dimensions={0,2,3,4} | broadcast | bytes 20643840 | tf_op jit(solution)/shard_map/tile | solution.py:51
  30.5 7.4 %all-to-all-start = ((bf16[3,8,896,320]{2,3,0,1:T(8,128)(2,1)}), bf16[3,8,896,320]{2,3,0,1:T(8,128)(2,1)}, u32[]{:S(2)}, u32[]{:S(2)}) async-start(bf16[3,8,896,320]{2,3,0,1:T(8,128)(2,1)} %bitcast.59), calls=%async_computation | async-start | bytes 27525120 | tf_op jit(solution)/shard_map/all_to_all | solution.py:52
  38.0 2.0 collective-permute-start.2
  40.1 108.7 %collective-permute-done.2 = bf16[128,8]{0,1:T(8,128)(2,1)S(1)} collective-permute-done((bf16[128,8]{0,1:T(8,128)(2,1)S(1)}, bf16[128,8]{0,1:T(8,128)(2,1)S(1)}, u32[]{:S(2)}, u32[]{:S(2)}) %collective-permute-start.2) | collective-permute-done | bytes 2080 | tf_op jit(solution)/shard_map/ppermute | solution.py:24
  148.8 1.7 collective-permute-start.3
  150.9 2.5 all_gather.3
  153.3 2.5 collective-permute-start.4
  156.4 104.2 %collective-permute-done.3 = bf16[256,8]{0,1:T(8,128)(2,1)S(1)} collective-permute-done((bf16[256,8]{0,1:T(8,128)(2,1)S(1)}, bf16[256,8]{0,1:T(8,128)(2,1)S(1)}, u32[]{:S(2)}, u32[]{:S(2)}) %collective-permute-start.3) | collective-permute-done | bytes 4128 | tf_op jit(solution)/shard_map/ppermute | solution.py:24
  262.7 1.9 maximum_select_fusion.1
  264.6 2.5 collective-permute-start.5
  267.7 1.4 gather_fusion
  271.1 104.5 %collective-permute-done.5 = bf16[256,3584]{1,0:T(8,128)(2,1)} collective-permute-done((bf16[256,3584]{1,0:T(8,128)(2,1)S(1)}, bf16[256,3584]{1,0:T(8,128)(2,1)}, u32[]{:S(2)}, u32[]{:S(2)}) %collective-permute-start.5) | collective-permute-done | bytes 1835040 | tf_op jit(solution)/shard_map/ppermute | solution.py:24
  375.6 3.8 maximum_select_fusion
  379.4 4.5 gather_fusion.1
  383.9 4.5 gather_fusion.3
  388.5 8.6 %copy.27 = bf16[8,3,40,8,896]{4,3,0,2,1:T(8,128)(2,1)S(1)} copy(bf16[8,3,40,8,896]{4,3,2,1,0:T(8,128)(2,1)} %bitcast.20) | data formatting | bytes 27525120 | tf_op jit(solution)/shard_map/reshape | solution.py:53
  397.8 4.2 copy-done
  402.8 5.9 %convolution_multiply_fusion.1 = f32[128,3584]{1,0:T(8,128)} fusion(bf16[3,7168,320]{1,2,0:T(8,128)(2,1)} %bitcast.62, f32[128]{0:T(128)S(1)} %broadcast_select_fusion.1, f32[128,320]{0,1:T(8,128)S(1)} %fusion.4, bf16[128,3584]{1,0:T(8,128)(2,1)S(1)} %gather_fusion.1), kind=kOutput, calls=%fused_computation.8 | convolution fusion | flops 587907072 | bytes 7504384 | tf_op jit(solution)/shard_map/dot_general | solution.py:83
  408.7 7.2 %scatter_custom_fusion = f32[512,3584]{1,0:T(8,128)} fusion(s32[128]{0:T(128)S(1)} %fusion.18, f32[128,3584]{1,0:T(8,128)} %convolution_multiply_fusion.1, f32[]{:T(128)} %constant.44.clone.1), kind=kCustom, calls=%fused_computation.10 | custom fusion | flops 458752 | bytes 7340544 | tf_op jit(solution)/shard_map/scatter-add | solution.py:86
  415.9 4.6 convolution_multiply_fusion
  420.6 8.9 %scatter_fusion = f32[512,3584]{1,0:T(8,128)} fusion(f32[512,3584]{1,0:T(8,128)} %scatter_custom_fusion, s32[128]{0:T(128)S(1)} %fusion.19, f32[128,3584]{1,0:T(8,128)S(1)} %convolution_multiply_fusion), kind=kCustom, calls=%fused_computation.5 | custom fusion | flops 458752 | bytes 5505536 | tf_op jit(solution)/shard_map/scatter-add | solution.py:86
  429.4 5.3 %convert_element_type.57 = bf16[512,3584]{1,0:T(8,128)(2,1)} convert(f32[512,3584]{1,0:T(8,128)} %scatter_fusion) | non-fusion elementwise | flops 1835008 | bytes 11010048 | tf_op jit(solution)/shard_map/convert_element_type | solution.py:87
  434.7 10.8 %reduce-scatter.2.cloned.1.call-done = bf16[512,1792]{1,0:T(8,128)(2,1)} async-done(((bf16[512,3584]{1,0:T(8,128)(2,1)}), bf16[512,1792]{1,0:T(8,128)(2,1)}) %reduce-scatter.2.cloned.1.call-update) | async-done | bytes 1835024 | tf_op jit(solution)/shard_map/reduce_scatter | solution.py:88
  445.5 1.8 convert_element_type.58
  447.5 1.9 collective-permute-start.6
  449.4 20.7 %collective-permute-done.6 = bf16[256,1792]{1,0:T(8,128)(2,1)S(1)} collective-permute-done((bf16[256,1792]{1,0:T(8,128)(2,1)S(1)}, bf16[256,1792]{1,0:T(8,128)(2,1)S(1)}, u32[]{:S(2)}, u32[]{:S(2)}) %collective-permute-start.6) | collective-permute-done | bytes 917536 | tf_op jit(solution)/shard_map/ppermute | solution.py:24
  470.4 1.7 collective-permute-start.7
  472.2 10.2 %collective-permute-done.7 = bf16[128,1792]{1,0:T(8,128)(2,1)S(1)} collective-permute-done((bf16[128,1792]{1,0:T(8,128)(2,1)S(1)}, bf16[128,1792]{1,0:T(8,128)(2,1)S(1)}, u32[]{:S(2)}, u32[]{:S(2)}) %collective-permute-start.7) | collective-permute-done | bytes 458784 | tf_op jit(solution)/shard_map/ppermute | solution.py:24
  (58 shorter events, 9.0 us)
Async XLA Ops:
  6.5 4.6 copy-start.1
  30.5 7.5 %copy-start.3 = (f32[128,8]{0,1:T(8,128)S(1)}, f32[128,8]{0,1:T(8,128)}, u32[]{:S(2)}) copy-start(f32[128,8]{0,1:T(8,128)} %param.9) | copy-start | bytes 12292
  30.5 9.5 %copy-start.4 = (s32[128,8]{0,1:T(8,128)S(1)}, s32[128,8]{0,1:T(8,128)}, u32[]{:S(2)}) copy-start(s32[128,8]{0,1:T(8,128)} %param.8) | copy-start | bytes 12292
  30.5 120.4 %copy-start.2 = (bf16[128,1792]{1,0:T(8,128)(2,1)S(1)}, bf16[128,1792]{1,0:T(8,128)(2,1)}, u32[]{:S(2)}) copy-start(bf16[128,1792]{1,0:T(8,128)(2,1)} %param.7) | copy-start | bytes 1376260
  30.5 125.3 %copy-start.5 = (s32[2]{0:T(128)S(1)}, s32[2]{0:T(128)}, u32[]{:S(2)}) copy-start(s32[2]{0:T(128)} %param.10) | copy-start | bytes 28
  30.5 358.0 %all-to-all-start = ((bf16[3,8,896,320]{2,3,0,1:T(8,128)(2,1)}), bf16[3,8,896,320]{2,3,0,1:T(8,128)(2,1)}, u32[]{:S(2)}, u32[]{:S(2)}) async-start(bf16[3,8,896,320]{2,3,0,1:T(8,128)(2,1)} %bitcast.59), calls=%async_computation | async-start | bytes 27525120 | tf_op jit(solution)/shard_map/all_to_all | solution.py:52
  37.9 407.6 %reduce-scatter.2.cloned.1.call-start = ((), (), s32[]{:S(2)}) async-start(), calls=%async_computation.2 | async-start | bytes 5505024 | tf_op jit(solution)/shard_map/reduce_scatter | solution.py:88
  38.0 110.9 %collective-permute-start.2 = (bf16[128,8]{0,1:T(8,128)(2,1)S(1)}, bf16[128,8]{0,1:T(8,128)(2,1)S(1)}, u32[]{:S(2)}, u32[]{:S(2)}) collective-permute-start(bf16[128,8]{0,1:T(8,128)(2,1)S(1)} %convert_element_type.50), channel_id=1, source_target_pairs={{0,2},{2,0},{4,6},{6,4},{8,10},{10,8},{12,14},{14,12},{1,3},{3,1},... | collective-permute-start | bytes 6152 | tf_op jit(solution)/shard_map/ppermute | solution.py:24
  40.0 110.6 %collective-permute-start = (s32[128,8]{0,1:T(8,128)S(1)}, s32[128,8]{0,1:T(8,128)S(1)}, u32[]{:S(2)}, u32[]{:S(2)}) collective-permute-start(s32[128,8]{0,1:T(8,128)S(1)} %copy-done.4), channel_id=1, source_target_pairs={{0,2},{2,0},{4,6},{6,4},{8,10},{10,8},{12,14},{14,12},{1,3},{3,1},... | collective-permute-start | bytes 12296 | tf_op jit(solution)/shard_map/ppermute | solution.py:24
  148.8 111.8 %collective-permute-start.3 = (bf16[256,8]{0,1:T(8,128)(2,1)S(1)}, bf16[256,8]{0,1:T(8,128)(2,1)S(1)}, u32[]{:S(2)}, u32[]{:S(2)}) collective-permute-start(bf16[256,8]{0,1:T(8,128)(2,1)S(1)} %get-tuple-element.10), channel_id=1, source_target_pairs={{0,4},{2,6},{4,0},{6,2},{8,12},{10,14},{12,8},{14,10},{1,5},{3,7},... | collective-permute-start | bytes 12296 | tf_op jit(solution)/shard_map/ppermute | solution.py:24
  150.6 110.1 %collective-permute-start.1 = (s32[256,8]{0,1:T(8,128)S(1)}, s32[256,8]{0,1:T(8,128)S(1)}, u32[]{:S(2)}, u32[]{:S(2)}) collective-permute-start(s32[256,8]{0,1:T(8,128)S(1)} %add_select_fusion.1), channel_id=1, source_target_pairs={{0,4},{2,6},{4,0},{6,2},{8,12},{10,14},{12,8},{14,10},{1,5},{3,7},... | collective-permute-start | bytes 24584 | tf_op jit(solution)/shard_map/ppermute | solution.py:24
  153.3 109.3 %collective-permute-start.4 = (bf16[128,3584]{1,0:T(8,128)(2,1)S(1)}, bf16[128,3584]{1,0:T(8,128)(2,1)}, u32[]{:S(2)}, u32[]{:S(2)}) collective-permute-start(bf16[128,3584]{1,0:T(8,128)(2,1)S(1)} %all_gather.3), channel_id=1, source_target_pairs={{0,2},{2,0},{4,6},{6,4},{8,10},{10,8},{12,14},{14,12},{1,3},{3,1},... | collective-permute-start | bytes 2752520 | tf_op jit(solution)/shard_map/ppermute | solution.py:24
  264.6 110.9 %collective-permute-start.5 = (bf16[256,3584]{1,0:T(8,128)(2,1)S(1)}, bf16[256,3584]{1,0:T(8,128)(2,1)}, u32[]{:S(2)}, u32[]{:S(2)}) collective-permute-start(bf16[256,3584]{1,0:T(8,128)(2,1)S(1)} %maximum_select_fusion.1), channel_id=1, source_target_pairs={{0,4},{2,6},{4,0},{6,2},{8,12},{10,14},{12,8},{14,10},{1,5},{3,7},... | collective-permute-start | bytes 5505032 | tf_op jit(solution)/shard_map/ppermute | solution.py:24
  397.1 4.9 %copy-start = (bf16[8,3,40,8,896]{4,3,0,2,1:T(8,128)(2,1)}, bf16[8,3,40,8,896]{4,3,0,2,1:T(8,128)(2,1)S(1)}, u32[]{:S(2)}) copy-start(bf16[8,3,40,8,896]{4,3,0,2,1:T(8,128)(2,1)S(1)} %copy.27) | copy-start | bytes 41287684
  447.5 22.7 %collective-permute-start.6 = (bf16[256,1792]{1,0:T(8,128)(2,1)S(1)}, bf16[256,1792]{1,0:T(8,128)(2,1)S(1)}, u32[]{:S(2)}, u32[]{:S(2)}) collective-permute-start(bf16[256,1792]{1,0:T(8,128)(2,1)S(1)} %select_convert_fusion), channel_id=1, source_target_pairs={{0,4},{2,6},{4,0},{6,2},{8,12},{10,14},{12,8},{14,10},{1,5},{3,7},... | collective-permute-start | bytes 2752520 | tf_op jit(solution)/shard_map/ppermute | solution.py:24
  470.4 12.0 %collective-permute-start.7 = (bf16[128,1792]{1,0:T(8,128)(2,1)S(1)}, bf16[128,1792]{1,0:T(8,128)(2,1)S(1)}, u32[]{:S(2)}, u32[]{:S(2)}) collective-permute-start(bf16[128,1792]{1,0:T(8,128)(2,1)S(1)} %select_convert_fusion.1), channel_id=1, source_target_pairs={{0,2},{2,0},{4,6},{6,4},{8,10},{10,8},{12,14},{14,12},{1,3},{3,1},... | collective-permute-start | bytes 1376264 | tf_op jit(solution)/shard_map/ppermute | solution.py:24
Sparse Core Ops, SparseCore 0:
  434.8 10.6 reduce-scatter.1
where the time goes:
time: 491 us; the launch traced here: 490 us
  waiting for transfers between devices  359 us (73%)
  local copies, waits for them, and re-layouts  45.6 us (9%)
  other arithmetic  36.9 us (8%)
  starting transfers between devices  20.3 us (4%)
  between operations  13.6 us (3%)
  matrix products  12.1 us (2%)
    ppermute x8, waiting for transfers between devices, swapped(): lax.ppermute(array, axis, [(i, i ^ 1 << distance) for i in range(lax.axis...  348 us
    unnamed x15, local copies, waits for them, and re-layouts  16.3 us
    scatter-add x2, other arithmetic, shards(): partials = partials.at[slot_rows].add(slot_weight[:, None] * projected)  16.1 us
    ppermute x8, starting transfers between devices, swapped(): lax.ppermute(array, axis, [(i, i ^ 1 << distance) for i in range(lax.axis...  12.8 us
    reduce_scatter x1, waiting for transfers between devices, shards(): lax.psum_scatter(rounded.astype(jnp.bfloat16), 'tp', scatter_dimension=1,...  10.8 us
    dot_general x2, matrix products, shards(): lax.dot_general(hidden, down_cols, (((1,), (1,)), ((), ())), preferred_el...  10.6 us
  transfers between devices with their start and end apart: 10, of which 6 were waited for; matrix products, arithmetic and copies ran while one was open for 4% of the time, Pallas kernels for 0%

commit v1 on v0

--- a/solution.py
+++ b/solution.py
@@ -1,6 +1,10 @@
+import functools
+
 import jax
 import jax.numpy as jnp
 from jax import lax
+from jax.experimental import pallas as pl
+from jax.experimental.pallas import tpu as pltpu
 from jax.sharding import PartitionSpec as P
 
 D = 3584
@@ -8,6 +12,7 @@
 WAVE = 2
 MEMBERS = 8
 GROUP_EP = 4
+MESH = pl.DeviceIdType.MESH
 TOK_G = 512
 CAP = 128
 
@@ -99,6 +104,380 @@
     return halved.astype(jnp.bfloat16)
 
 
+def dot(a, b, dims=((1,), (0,))):
+    return lax.dot_general(a, b, (dims, ((), ())), preferred_element_type=jnp.float32)
+
+
+def owner_kernel(
+    owners,
+    info_ref,
+    tok_ref,
+    gate_ref,
+    up_ref,
+    down_ref,
+    out_ref,
+    info_all,
+    rows_in,
+    route,
+    scat,
+    row_w,
+    x_own,
+    x_far,
+    gate_v,
+    up_v,
+    down_v,
+    part_out,
+    part_in,
+    hid,
+    proj_out,
+    proj_in,
+    proj_own,
+    fin,
+    fin_in,
+    dense,
+    w_sem,
+    info_send,
+    info_recv,
+    tok_send,
+    tok_recv,
+    xa_sem,
+    xb_sem,
+    xf_sem,
+    rs_send,
+    rs_recv,
+    ag_send,
+    ag_recv,
+    tp_send,
+    tp_recv,
+    far_sem,
+    out_send,
+    out_recv,
+):
+    ep = lax.axis_index("ep")
+    t = lax.axis_index("tp")
+    other_t = 1 - t
+    group = ep // owners
+    k = ep % owners
+    base = group * owners
+    far_ep = (1 - group) * owners + k
+    width = tok_ref.shape[2]
+    tok_rows = tok_ref.shape[1]
+    share = part_in.shape[3]
+
+    loads = [
+        pltpu.make_async_copy(src, dst, w_sem.at[i])
+        for i, (src, dst) in enumerate(
+            ((gate_ref, gate_v), (up_ref, up_v), (down_ref, down_v))
+        )
+    ]
+    for load in loads:
+        load.start()
+
+    barrier = pltpu.get_barrier_semaphore()
+    for step in range(1, owners):
+        peer = base + (k + step) % owners
+        for side in range(2):
+            pl.semaphore_signal(
+                barrier, inc=1, device_id={"ep": peer, "tp": side}, device_id_type=MESH
+            )
+    pl.semaphore_signal(barrier, inc=1, device_id={"tp": other_t}, device_id_type=MESH)
+    pl.semaphore_signal(barrier, inc=1, device_id={"ep": far_ep}, device_id_type=MESH)
+    pl.semaphore_wait(barrier, 2 * owners)
+
+    def remote(src, dst, send, recv, where):
+        return pltpu.make_async_remote_copy(
+            src_ref=src,
+            dst_ref=dst,
+            send_sem=send,
+            recv_sem=recv,
+            device_id=where,
+            device_id_type=MESH,
+        )
+
+    info_copies = [
+        remote(
+            info_ref,
+            info_all.at[k],
+            info_send.at[step - 1],
+            info_recv.at[step - 1],
+            {"ep": base + (k + step) % owners},
+        )
+        for step in range(1, owners)
+    ]
+    for copy in info_copies:
+        copy.start()
+
+    tok_copies = []
+    for block in range(4):
+        to_k = 2 * t + block // 2
+        to_t = block % 2
+        mine = jnp.logical_and(k == to_k, t == to_t)
+        tok_copies.append(
+            (
+                mine,
+                remote(
+                    tok_ref.at[block],
+                    rows_in.at[k],
+                    tok_send.at[block],
+                    tok_recv.at[k],
+                    {"ep": base + to_k, "tp": to_t},
+                ),
+            )
+        )
+
+        @pl.when(jnp.logical_not(mine))
+        def _(copy=tok_copies[-1][1]):
+            copy.start()
+
+        @pl.when(mine)
+        def _(block=block):
+            pltpu.make_async_copy(tok_ref.at[block], rows_in.at[k], tok_recv.at[k]).start()
+
+    info_all[k] = info_ref[...]
+    size = owners * tok_rows
+    before = jnp.where(
+        lax.broadcasted_iota(jnp.int32, (size, size), 0)
+        < lax.broadcasted_iota(jnp.int32, (size, size), 1),
+        1.0,
+        0.0,
+    ).astype(jnp.bfloat16)
+    for copy in info_copies:
+        copy.wait_recv()
+    weights = jnp.concatenate([info_all[j] for j in range(owners)], axis=1)
+    chosen = jnp.where(weights > 0.0, 1.0, 0.0)
+    pad = jnp.concatenate([chosen, chosen], axis=0).astype(jnp.bfloat16)
+    place = dot(pad, before)[: weights.shape[0]]
+    place = jnp.where(weights > 0.0, place, -1.0)
+    first = group == 0
+    near_place = jnp.where(first, place[0:1], place[1:2])
+    far_place = jnp.where(first, place[1:2], place[0:1])
+    near_w = jnp.where(first, weights[0:1], weights[1:2])
+    far_w = jnp.where(first, weights[1:2], weights[0:1])
+    slots = lax.broadcasted_iota(jnp.int32, (CAP, size), 0).astype(jnp.float32)
+    route[0] = jnp.where(near_place == slots, 1.0, 0.0).astype(jnp.bfloat16)
+    route[1] = jnp.where(far_place == slots, 1.0, 0.0).astype(jnp.bfloat16)
+
+    for j in range(owners):
+        pltpu.make_async_copy(tok_ref.at[0], rows_in.at[j], tok_recv.at[j]).wait()
+    rows = rows_in[...].reshape(size, width)
+    x_far_out = x_far.at[2]
+    x_far_out[...] = dot(route[1], rows).astype(jnp.bfloat16)
+    far_x = remote(x_far_out, x_far.at[t], xb_sem.at[0], xb_sem.at[1], {"ep": far_ep})
+    far_x.start()
+    x_own[t] = dot(route[0], rows).astype(jnp.bfloat16)
+    own_x = remote(x_own.at[t], x_own.at[t], xa_sem.at[0], xa_sem.at[1], {"tp": other_t})
+    own_x.start()
+
+    def both(first_rows):
+        return pl.ds(pl.multiple_of(first_rows * width, 16), width)
+
+    for load in loads[:2]:
+        load.wait()
+
+    def spread(half, x_ref, wait_partner):
+        near, away = both(t), both(other_t)
+        gate = dot(x_ref[t], gate_v[near])
+        up = dot(x_ref[t], up_v[near])
+        wait_partner()
+        gate = (gate + dot(x_ref[other_t], gate_v[away])).astype(jnp.bfloat16)
+        up = (up + dot(x_ref[other_t], up_v[away])).astype(jnp.bfloat16)
+        for j in range(owners):
+            part_out[half, j, 0] = gate[j * share : (j + 1) * share]
+            part_out[half, j, 1] = up[j * share : (j + 1) * share]
+        copies = []
+        for step in range(1, owners):
+            to = (k + step) % owners
+            copies.append(
+                remote(
+                    part_out.at[half, to],
+                    part_in.at[half, step - 1],
+                    rs_send.at[half, step - 1],
+                    rs_recv.at[half, step - 1],
+                    {"ep": base + to},
+                )
+            )
+            copies[-1].start()
+        return copies
+
+    def activate(half, arriving):
+        gate = part_out[half, k, 0].astype(jnp.float32)
+        up = part_out[half, k, 1].astype(jnp.float32)
+        for step in range(1, owners):
+            arriving[step - 1].wait_recv()
+            gate = gate + part_in[half, step - 1, 0].astype(jnp.float32)
+            up = up + part_in[half, step - 1, 1].astype(jnp.float32)
+        hid[half, k] = (gate / (1.0 + jnp.exp(-gate)) * up).astype(jnp.bfloat16)
+        copies = []
+        for step in range(1, owners):
+            copies.append(
+                remote(
+                    hid.at[half, k],
+                    hid.at[half, k],
+                    ag_send.at[half, step - 1],
+                    ag_recv.at[half, step - 1],
+                    {"ep": base + (k + step) % owners},
+                )
+            )
+            copies[-1].start()
+        return copies
+
+    def project(half, arriving):
+        for copy in arriving:
+            copy.wait_recv()
+        hidden = hid[half].reshape(CAP, hid.shape[3])
+        proj_out[half] = dot(hidden, down_v[both(other_t)], ((1,), (1,))).astype(jnp.bfloat16)
+        copy = remote(
+            proj_out.at[half],
+            proj_in.at[half],
+            tp_send.at[half],
+            tp_recv.at[half],
+            {"tp": other_t},
+        )
+        copy.start()
+        proj_own[half] = dot(hidden, down_v[both(t)], ((1,), (1,)))
+        return copy
+
+    def settle(half, copy):
+        copy.wait_recv()
+        fin[half] = (proj_own[half] + proj_in[half].astype(jnp.float32)).astype(jnp.bfloat16)
+
+    rs_a = spread(0, x_own, own_x.wait_recv)
+
+    columns = jnp.transpose(
+        jnp.concatenate([near_place, far_place, near_w, far_w, weights[: 8 - 4]], axis=0)
+    )
+    row_w[...] = columns
+    lanes = lax.broadcasted_iota(jnp.int32, (size, CAP), 1).astype(jnp.float32)
+    scat[0] = jnp.where(columns[:, 0:1] == lanes, 1.0, 0.0).astype(jnp.bfloat16)
+    scat[1] = jnp.where(columns[:, 1:2] == lanes, 1.0, 0.0).astype(jnp.bfloat16)
+
+    far_x.wait_recv()
+    pass_x = remote(x_far.at[t], x_far.at[t], xf_sem.at[0], xf_sem.at[1], {"tp": other_t})
+    pass_x.start()
+    rs_b = spread(1, x_far, pass_x.wait_recv)
+    ag_a = activate(0, rs_a)
+    ag_b = activate(1, rs_b)
+    loads[2].wait()
+    tp_a = project(0, ag_a)
+    settle(0, tp_a)
+    tp_b = project(1, ag_b)
+    settle(1, tp_b)
+    far_y = remote(fin.at[1], fin_in, far_sem.at[0], far_sem.at[1], {"ep": far_ep})
+    far_y.start()
+    near_y = [
+        row_w[pl.ds(j * tok_rows, tok_rows), 2:3]
+        * dot(scat[0, pl.ds(j * tok_rows, tok_rows)], fin[0])
+        for j in range(owners)
+    ]
+    far_y.wait_recv()
+    spot = 2 * (k % 2) + t
+    to_t = k // 2
+    out_copies = []
+    for j in range(owners):
+        rows_j = pl.ds(j * tok_rows, tok_rows)
+        far_part = row_w[rows_j, 3:4] * dot(scat[1, rows_j], fin_in[...])
+        dense[j] = (near_y[j] + far_part).astype(jnp.bfloat16)
+        mine = jnp.logical_and(k == j, t == to_t)
+        copy = remote(
+            dense.at[j],
+            out_ref.at[spot],
+            out_send.at[j],
+            out_recv.at[spot],
+            {"ep": base + j, "tp": to_t},
+        )
+        out_copies.append((mine, copy))
+
+        @pl.when(jnp.logical_not(mine))
+        def _(copy=copy):
+            copy.start()
+
+        @pl.when(mine)
+        def _(j=j):
+            pltpu.make_async_copy(dense.at[j], out_ref.at[spot], out_recv.at[spot]).start()
+
+    for mine, copy in tok_copies + out_copies:
+
+        @pl.when(jnp.logical_not(mine))
+        def _(copy=copy):
+            copy.wait_send()
+
+    for copy in info_copies + rs_a + rs_b + ag_a + ag_b + [far_x, own_x, pass_x, tp_a, tp_b, far_y]:
+        copy.wait_send()
+    for block in range(4):
+        pltpu.make_async_copy(dense.at[0], out_ref.at[block], out_recv.at[block]).wait()
+
+
+def stay_shards(tokens, expert_ids, gate_values, group_counts, gate_weight, up_weight, down_weight):
+    ep_index = lax.axis_index("ep")
+    owners = lax.axis_size("ep") // WAVE
+    rows, features = tokens.shape
+    held, half_ff = gate_weight.shape
+    width = held // 2
+    blocks = features // width
+    live_count = lax.dynamic_index_in_dim(group_counts, ep_index // GROUP_EP, keepdims=False)
+    live = (ep_index % GROUP_EP) * rows + jnp.arange(rows, dtype=jnp.int32) < live_count
+    named = expert_ids[None] == jnp.arange(8, dtype=jnp.int32)[:, None, None]
+    named = jnp.logical_and(named, live[None, :, None])
+    info = jnp.sum(jnp.where(named, gate_values[None], jnp.float32(0.0)), axis=2)
+    cut = tokens.reshape(rows, blocks, width).transpose(1, 0, 2)
+    share = CAP // owners
+    size = owners * rows
+    bf16, f32 = jnp.bfloat16, jnp.float32
+    dma = pltpu.SemaphoreType.DMA
+    anywhere = pl.BlockSpec(memory_space=pl.ANY)
+    result = pl.pallas_call(
+        functools.partial(owner_kernel, owners),
+        out_shape=jax.ShapeDtypeStruct((blocks, rows, width), bf16),
+        in_specs=[pl.BlockSpec(memory_space=pltpu.VMEM)] + [anywhere] * 4,
+        out_specs=anywhere,
+        scratch_shapes=[
+            pltpu.VMEM((owners, 8, rows), f32),
+            pltpu.VMEM((owners, rows, width), bf16),
+            pltpu.VMEM((2, CAP, size), bf16),
+            pltpu.VMEM((2, size, CAP), bf16),
+            pltpu.VMEM((size, 8), f32),
+            pltpu.VMEM((2, CAP, width), bf16),
+            pltpu.VMEM((3, CAP, width), bf16),
+            pltpu.VMEM((held, half_ff), bf16),
+            pltpu.VMEM((held, half_ff), bf16),
+            pltpu.VMEM((held, half_ff), bf16),
+            pltpu.VMEM((2, owners, 2, share, half_ff), bf16),
+            pltpu.VMEM((2, owners - 1, 2, share, half_ff), bf16),
+            pltpu.VMEM((2, owners, share, half_ff), bf16),
+            pltpu.VMEM((2, CAP, width), bf16),
+            pltpu.VMEM((2, CAP, width), bf16),
+            pltpu.VMEM((2, CAP, width), f32),
+            pltpu.VMEM((2, CAP, width), bf16),
+            pltpu.VMEM((CAP, width), bf16),
+            pltpu.VMEM((owners, rows, width), bf16),
+            dma((3,)),
+            dma((owners - 1,)),
+            dma((owners - 1,)),
+            dma((4,)),
+            dma((owners,)),
+            dma((2,)),
+            dma((2,)),
+            dma((2,)),
+            dma((2, owners - 1)),
+            dma((2, owners - 1)),
+            dma((2, owners - 1)),
+            dma((2, owners - 1)),
+            dma((2,)),
+            dma((2,)),
+            dma((2,)),
+            dma((owners,)),
+            dma((4,)),
+        ],
+        compiler_params=pltpu.CompilerParams(collective_id=0, has_side_effects=True),
+    )(info, cut, gate_weight, up_weight, down_weight)
+    return result.transpose(1, 0, 2).reshape(rows, features)
+
+
+def shards_for(mesh):
+    whole_owners = mesh.shape["ep"] == WAVE * GROUP_EP and mesh.shape["tp"] == 2
+    return stay_shards if whole_owners else shards
+
+
 def solution(mesh):
     placed = (
         P(("rep", "ep"), "tp"),
@@ -110,5 +489,5 @@
         P(("rep", "ep"), "tp"),
     )
     return jax.shard_map(
-        shards, mesh=mesh, in_specs=placed, out_specs=P(("rep", "ep"), "tp"), check_vma=False
+        shards_for(mesh), mesh=mesh, in_specs=placed, out_specs=P(("rep", "ep"), "tp"), check_vma=False
     )

time: 491 us -> 64.1 us (0.13)
  waiting for transfers between devices: 359 us -> 0 us
  Pallas kernels: 0 us -> 56 us
  local copies, waits for them, and re-layouts: 45.6 us -> 5.81 us
  other arithmetic: 36.9 us -> 1.96 us
  starting transfers between devices: 20.3 us -> 0 us
  between operations: 13.6 us -> 0.02 us
  matrix products: 12.1 us -> 0 us
    ppermute x8 -> x0, waiting for transfers between devices: 348 us -> none  [swapped(): lax.ppermute(array, axis, [(i, i ^ 1 << distance) for i in range(lax.axis...]
    pallas_call x0 -> x1, Pallas kernels: none -> 56 us  [stay_shards(): pl.pallas_call(functools.partial(owner_kernel, owners), out_shape=jax.Sha...]
    scatter-add x2 -> x0, other arithmetic: 16.1 us -> none  [shards(): partials = partials.at[slot_rows].add(slot_weight[:, None] * projected)]
    unnamed x15 -> x1, local copies, waits for them, and re-layouts: 16.3 us -> 1.27 us
    ppermute x8 -> x0, starting transfers between devices: 12.8 us -> none  [swapped(): lax.ppermute(array, axis, [(i, i ^ 1 << distance) for i in range(lax.axis...]
    dot_general x4 -> x0, matrix products: 12.1 us -> none  [the longest x2 10.6 us: shards(): lax.dot_general(hidden, down_cols, (((1,), (1,)), ((), ())), preferred_el...]
    gather x4 -> x0, local copies, waits for them, and re-layouts: 11.8 us -> none  [the longest x2 9.07 us: shards(): expert_rows = group_tokens[slot_rows]]
    reduce_scatter x1 -> x0, waiting for transfers between devices: 10.8 us -> none  [shards(): lax.psum_scatter(rounded.astype(jnp.bfloat16), 'tp', scatter_dimension=1,...]
  transfers between devices with their start and end apart: 10 -> 0, of which waited for: 6 -> 0; matrix products, arithmetic and copies ran while one was open for 4% -> 0% of each run, Pallas kernels for 0% -> 0%
where the time goes in v1:
time: 64.1 us; the launch traced here: 63.8 us
  Pallas kernels  56 us (87%)
  local copies, waits for them, and re-layouts  5.81 us (9%)
  other arithmetic  1.96 us (3%)
    pallas_call x1, Pallas kernels, stay_shards(): pl.pallas_call(functools.partial(owner_kernel, owners), out_shape=jax.Sha...  56 us
    reduce_sum x1, other arithmetic, stay_shards(): jnp.sum(jnp.where(named, gate_values[None], jnp.float32(0.0)), axis=2)  1.31 us
    transpose x1, local copies, waits for them, and re-layouts, stay_shards(): return result.transpose(1, 0, 2).reshape(rows, features)  1.3 us

profile of v1, /device:TPU:0, one launch (start us, length us, event | category | flops | bytes accessed | tf_op | source)
XLA Modules:
  0.0 63.8 jit_solution(3174588822225942149)
XLA Ops:
  0.0 1.2 %dynamic_slice.4 = s32[1]{0:T(128)} dynamic-slice(s32[2]{0:T(128)} %param.10, s32[]{:T(128)S(6)} %select_n.21), dynamic_slice_sizes={1} | dynamic-slice | bytes 12 | tf_op jit(solution)/shard_map/jit(dynamic_index_in_dim)/dynamic_slice | solution.py:417
  1.2 0.7 %add_compare_fusion = pred[128]{0:T(512)(128)(4,1)S(1)} fusion(s32[]{:T(128)} %bitcast, s32[]{:T(128)S(6)} %mul.3), kind=kLoop, calls=%fused_computation.3 | loop fusion | flops 256 | bytes 136 | tf_op jit(solution)/shard_map/lt | solution.py:418
  1.9 1.3 %select_reduce_fusion.info_ref = f32[8,128]{1,0:T(8,128)} fusion(f32[128,8]{0,1:T(8,128)} %param.9, s32[128,8]{0,1:T(8,128)} %param.8, pred[128]{0:T(512)(128)(4,1)S(1)} %add_compare_fusion), kind=kLoop, calls=%fused_computation | loop fusion | flops 31744 | bytes 12416 | tf_op jit(solution)/shard_map/reduce_sum | solution.py:421
  3.2 1.3 %copy.16 = bf16[128,1792]{0,1:T(8,128)(2,1)S(1)} copy(bf16[128,1792]{1,0:T(8,128)(2,1)} %param.7) | data formatting | bytes 917504 | tf_op args[0]
  4.5 1.0 %copy.17 = bf16[128,4,448]{2,0,1:T(8,128)(2,1)} copy(bf16[128,4,448]{0,2,1:T(8,128)(2,1)S(1)} %bitcast.8) | data formatting | bytes 917504 | tf_op jit(solution)/shard_map/reshape | solution.py:422
  5.5 56.0 %shard_map.73 = bf16[4,128,448]{2,1,0:T(8,128)(2,1)} custom-call(f32[8,128]{1,0:T(8,128)} %select_reduce_fusion.info_ref, bf16[4,128,448]{2,1,0:T(8,128)(2,1)} %bitcast.5, bf16[896,1280]{1,0:T(8,128)(2,1)} %gate_ref.1, bf16[896,1280]{1,0:T(8,128)(2,1)} %up_ref.1, bf16[896,1280]{1,0:T(8,128)(2,1)} %down_ref.1), custom_call_target="tpu_custom_call" | custom-call | tf_op jit(solution)/shard_map/pallas_call | solution.py:428
  61.5 1.3 %copy.18 = bf16[128,4,448]{0,2,1:T(8,128)(2,1)S(1)} copy(bf16[128,4,448]{2,0,1:T(8,128)(2,1)} %bitcast.6) | data formatting | bytes 917504 | tf_op jit(solution)/shard_map/transpose | solution.py:473
  62.8 1.0 %copy.19 = bf16[128,1792]{1,0:T(8,128)(2,1)} copy(bf16[128,1792]{0,1:T(8,128)(2,1)S(1)} %bitcast.7) | data formatting | bytes 917504 | tf_op jit(solution)/shard_map/reshape | solution.py:473

commit v2 on v1

--- a/solution.py
+++ b/solution.py
@@ -110,12 +110,15 @@
 
 def owner_kernel(
     owners,
-    info_ref,
+    count_ref,
+    ids_ref,
+    gates_ref,
     tok_ref,
     gate_ref,
     up_ref,
     down_ref,
     out_ref,
+    info,
     info_all,
     rows_in,
     route,
@@ -160,8 +163,11 @@
     k = ep % owners
     base = group * owners
     far_ep = (1 - group) * owners + k
-    width = tok_ref.shape[2]
-    tok_rows = tok_ref.shape[1]
+    tok_rows = tok_ref.shape[0]
+    held = gate_ref.shape[0]
+    window = x_own.shape[2]
+    shift = held - window
+    rest = shift
     share = part_in.shape[3]
 
     loads = [
@@ -172,6 +178,18 @@
     ]
     for load in loads:
         load.start()
+
+    ids = ids_ref[...]
+    row_at = lax.broadcasted_iota(jnp.int32, ids.shape, 1) + k * tok_rows
+    gates = jnp.where(row_at < count_ref[group], gates_ref[...], 0.0)
+    info[...] = jnp.concatenate(
+        [
+            jnp.sum(jnp.where(ids == expert, gates, 0.0), axis=0, keepdims=True)
+            for expert in range(WAVE)
+        ]
+        + [jnp.zeros((8 - WAVE, tok_rows), jnp.float32)],
+        axis=0,
+    )
 
     barrier = pltpu.get_barrier_semaphore()
     for step in range(1, owners):
@@ -196,7 +214,7 @@
 
     info_copies = [
         remote(
-            info_ref,
+            info,
             info_all.at[k],
             info_send.at[step - 1],
             info_recv.at[step - 1],
@@ -206,6 +224,9 @@
     ]
     for copy in info_copies:
         copy.start()
+
+    def window_of(block):
+        return tok_ref.at[:, pl.ds((block // 2) * held + (block % 2) * shift, window)]
 
     tok_copies = []
     for block in range(4):
@@ -216,7 +237,7 @@
             (
                 mine,
                 remote(
-                    tok_ref.at[block],
+                    window_of(block),
                     rows_in.at[k],
                     tok_send.at[block],
                     tok_recv.at[k],
@@ -231,9 +252,9 @@
 
         @pl.when(mine)
         def _(block=block):
-            pltpu.make_async_copy(tok_ref.at[block], rows_in.at[k], tok_recv.at[k]).start()
-
-    info_all[k] = info_ref[...]
+            pltpu.make_async_copy(window_of(block), rows_in.at[k], tok_recv.at[k]).start()
+
+    info_all[k] = info[...]
     size = owners * tok_rows
     before = jnp.where(
         lax.broadcasted_iota(jnp.int32, (size, size), 0)
@@ -258,8 +279,8 @@
     route[1] = jnp.where(far_place == slots, 1.0, 0.0).astype(jnp.bfloat16)
 
     for j in range(owners):
-        pltpu.make_async_copy(tok_ref.at[0], rows_in.at[j], tok_recv.at[j]).wait()
-    rows = rows_in[...].reshape(size, width)
+        pltpu.make_async_copy(window_of(0), rows_in.at[j], tok_recv.at[j]).wait()
+    rows = rows_in[...].reshape(size, window)
     x_far_out = x_far.at[2]
     x_far_out[...] = dot(route[1], rows).astype(jnp.bfloat16)
     far_x = remote(x_far_out, x_far.at[t], xb_sem.at[0], xb_sem.at[1], {"ep": far_ep})
@@ -268,19 +289,21 @@
     own_x = remote(x_own.at[t], x_own.at[t], xa_sem.at[0], xa_sem.at[1], {"tp": other_t})
     own_x.start()
 
-    def both(first_rows):
-        return pl.ds(pl.multiple_of(first_rows * width, 16), width)
+    def span(side):
+        return pl.ds(pl.multiple_of(side * shift, 128), window)
 
     for load in loads[:2]:
         load.wait()
 
     def spread(half, x_ref, wait_partner):
-        near, away = both(t), both(other_t)
+        near = span(t)
+        away = pl.ds(pl.multiple_of(other_t * window, 128), rest)
+        lanes = pl.ds(pl.multiple_of(other_t * (window - rest), 128), rest)
         gate = dot(x_ref[t], gate_v[near])
         up = dot(x_ref[t], up_v[near])
         wait_partner()
-        gate = (gate + dot(x_ref[other_t], gate_v[away])).astype(jnp.bfloat16)
-        up = (up + dot(x_ref[other_t], up_v[away])).astype(jnp.bfloat16)
+        gate = (gate + dot(x_ref[other_t, :, lanes], gate_v[away])).astype(jnp.bfloat16)
+        up = (up + dot(x_ref[other_t, :, lanes], up_v[away])).astype(jnp.bfloat16)
         for j in range(owners):
             part_out[half, j, 0] = gate[j * share : (j + 1) * share]
             part_out[half, j, 1] = up[j * share : (j + 1) * share]
@@ -325,7 +348,7 @@
         for copy in arriving:
             copy.wait_recv()
         hidden = hid[half].reshape(CAP, hid.shape[3])
-        proj_out[half] = dot(hidden, down_v[both(other_t)], ((1,), (1,))).astype(jnp.bfloat16)
+        proj_out[half] = dot(hidden, down_v[span(other_t)], ((1,), (1,))).astype(jnp.bfloat16)
         copy = remote(
             proj_out.at[half],
             proj_in.at[half],
@@ -334,7 +357,7 @@
             {"tp": other_t},
         )
         copy.start()
-        proj_own[half] = dot(hidden, down_v[both(t)], ((1,), (1,)))
+        proj_own[half] = dot(hidden, down_v[span(t)], ((1,), (1,)))
         return copy
 
     def settle(half, copy):
@@ -370,56 +393,62 @@
         for j in range(owners)
     ]
     far_y.wait_recv()
-    spot = 2 * (k % 2) + t
     to_t = k // 2
     out_copies = []
+    starts = (0, window)
+    sizes = (window, rest)
     for j in range(owners):
         rows_j = pl.ds(j * tok_rows, tok_rows)
         far_part = row_w[rows_j, 3:4] * dot(scat[1, rows_j], fin_in[...])
         dense[j] = (near_y[j] + far_part).astype(jnp.bfloat16)
-        mine = jnp.logical_and(k == j, t == to_t)
-        copy = remote(
-            dense.at[j],
-            out_ref.at[spot],
-            out_send.at[j],
-            out_recv.at[spot],
-            {"ep": base + j, "tp": to_t},
-        )
-        out_copies.append((mine, copy))
-
-        @pl.when(jnp.logical_not(mine))
-        def _(copy=copy):
-            copy.start()
-
-        @pl.when(mine)
-        def _(j=j):
-            pltpu.make_async_copy(dense.at[j], out_ref.at[spot], out_recv.at[spot]).start()
-
-    for mine, copy in tok_copies + out_copies:
-
-        @pl.when(jnp.logical_not(mine))
+        for side in range(2):
+            from_lanes = pl.ds(window - sizes[side], sizes[side])
+            for part in range(2):
+                picked = jnp.logical_and(t == side, k % 2 == part)
+                mine = jnp.logical_and(k == j, t == to_t)
+                to_lanes = pl.ds(part * held + starts[side], sizes[side])
+                spot = 2 * part + side
+                away = jnp.logical_and(picked, jnp.logical_not(mine))
+                copy = remote(
+                    dense.at[j, :, from_lanes],
+                    out_ref.at[:, to_lanes],
+                    out_send.at[j],
+                    out_recv.at[spot],
+                    {"ep": base + j, "tp": to_t},
+                )
+                out_copies.append((away, copy))
+
+                @pl.when(away)
+                def _(copy=copy):
+                    copy.start()
+
+                @pl.when(jnp.logical_and(picked, mine))
+                def _(j=j, from_lanes=from_lanes, to_lanes=to_lanes, spot=spot):
+                    pltpu.make_async_copy(
+                        dense.at[j, :, from_lanes], out_ref.at[:, to_lanes], out_recv.at[spot]
+                    ).start()
+
+    for away, copy in [(jnp.logical_not(mine), copy) for mine, copy in tok_copies] + out_copies:
+
+        @pl.when(away)
         def _(copy=copy):
             copy.wait_send()
 
     for copy in info_copies + rs_a + rs_b + ag_a + ag_b + [far_x, own_x, pass_x, tp_a, tp_b, far_y]:
         copy.wait_send()
-    for block in range(4):
-        pltpu.make_async_copy(dense.at[0], out_ref.at[block], out_recv.at[block]).wait()
+    for part in range(2):
+        for side in range(2):
+            here = pl.ds(part * held + starts[side], sizes[side])
+            pltpu.make_async_copy(
+                dense.at[0, :, pl.ds(0, sizes[side])], out_ref.at[:, here], out_recv.at[2 * part + side]
+            ).wait()
 
 
 def stay_shards(tokens, expert_ids, gate_values, group_counts, gate_weight, up_weight, down_weight):
-    ep_index = lax.axis_index("ep")
     owners = lax.axis_size("ep") // WAVE
     rows, features = tokens.shape
     held, half_ff = gate_weight.shape
-    width = held // 2
-    blocks = features // width
-    live_count = lax.dynamic_index_in_dim(group_counts, ep_index // GROUP_EP, keepdims=False)
-    live = (ep_index % GROUP_EP) * rows + jnp.arange(rows, dtype=jnp.int32) < live_count
-    named = expert_ids[None] == jnp.arange(8, dtype=jnp.int32)[:, None, None]
-    named = jnp.logical_and(named, live[None, :, None])
-    info = jnp.sum(jnp.where(named, gate_values[None], jnp.float32(0.0)), axis=2)
-    cut = tokens.reshape(rows, blocks, width).transpose(1, 0, 2)
+    width = (held // 2 + 127) // 128 * 128
     share = CAP // owners
     size = owners * rows
     bf16, f32 = jnp.bfloat16, jnp.float32
@@ -427,10 +456,16 @@
     anywhere = pl.BlockSpec(memory_space=pl.ANY)
     result = pl.pallas_call(
         functools.partial(owner_kernel, owners),
-        out_shape=jax.ShapeDtypeStruct((blocks, rows, width), bf16),
-        in_specs=[pl.BlockSpec(memory_space=pltpu.VMEM)] + [anywhere] * 4,
+        out_shape=jax.ShapeDtypeStruct((rows, features), bf16),
+        in_specs=[
+            pl.BlockSpec(memory_space=pltpu.SMEM),
+            pl.BlockSpec(memory_space=pltpu.VMEM),
+            pl.BlockSpec(memory_space=pltpu.VMEM),
+        ]
+        + [anywhere] * 4,
         out_specs=anywhere,
         scratch_shapes=[
+            pltpu.VMEM((8, rows), f32),
             pltpu.VMEM((owners, 8, rows), f32),
             pltpu.VMEM((owners, rows, width), bf16),
             pltpu.VMEM((2, CAP, size), bf16),
@@ -469,8 +504,8 @@
             dma((4,)),
         ],
         compiler_params=pltpu.CompilerParams(collective_id=0, has_side_effects=True),
-    )(info, cut, gate_weight, up_weight, down_weight)
-    return result.transpose(1, 0, 2).reshape(rows, features)
+    )(group_counts, expert_ids.T, gate_values.T, tokens, gate_weight, up_weight, down_weight)
+    return result
 
 
 def shards_for(mesh):

time: 64.1 us -> 57.5 us (0.90)
  local copies, waits for them, and re-layouts: 5.81 us -> 1.82 us
  other arithmetic: 1.96 us -> 0 us
    reshape x2 -> x0, local copies, waits for them, and re-layouts: 2 us -> none  [the longest x1 1.01 us: stay_shards(): cut = tokens.reshape(rows, blocks, width).transpose(1, 0, 2)]
    reduce_sum x1 -> x0, other arithmetic: 1.31 us -> none  [stay_shards(): jnp.sum(jnp.where(named, gate_values[None], jnp.float32(0.0)), axis=2)]
    transpose x1 -> x0, local copies, waits for them, and re-layouts: 1.3 us -> none  [stay_shards(): return result.transpose(1, 0, 2).reshape(rows, features)]
    dynamic_slice x1 -> x0, local copies, waits for them, and re-layouts: 1.24 us -> none  [stay_shards(): lax.dynamic_index_in_dim(group_counts, ep_index // GROUP_EP, keepdims=False)]
    lt x1 -> x0, other arithmetic: 0.65 us -> none  [stay_shards(): ep_index % GROUP_EP * rows + jnp.arange(rows, dtype=jnp.int32) < live_count]
where the time goes in v2:
time: 57.5 us; the launch traced here: 57.3 us
  Pallas kernels  55.5 us (97%)
  local copies, waits for them, and re-layouts  1.82 us (3%)
    pallas_call x1, Pallas kernels, stay_shards(): pl.pallas_call(functools.partial(owner_kernel, owners), out_shape=jax.Sha...  55.5 us
    unnamed x1, local copies, waits for them, and re-layouts  1.82 us

profile of v2, /device:TPU:0, one launch (start us, length us, event | category | flops | bytes accessed | tf_op | source)
XLA Modules:
  0.0 57.3 jit_solution(2894084135322252834)
XLA Ops:
  0.0 55.5 %shard_map.73 = bf16[128,1792]{1,0:T(8,128)(2,1)} custom-call(s32[2]{0:T(128)} %count_ref.1, s32[8,128]{1,0:T(8,128)} %bitcast.2, f32[8,128]{1,0:T(8,128)} %bitcast.3, bf16[128,1792]{1,0:T(8,128)(2,1)} %tok_ref.1, bf16[896,1280]{1,0:T(8,128)(2,1)} %gate_ref.1, bf16[896,1280]{1,0:T(8,128)(2,1)} %up_ref.1, bf16[896,1280]{1,0:T(8,128)(2,1)} %down_ref.1), custom_call_target="tpu_custom_call" | custom-call | tf_op jit(solution)/shard_map/pallas_call | solution.py:457
  55.5 1.8 %copy.9 = bf16[128,1792]{1,0:T(8,128)(2,1)} copy(bf16[128,1792]{1,0:T(8,128)(2,1)} %shard_map.73) | data formatting | bytes 917504

commit v3 on v2

--- a/solution.py
+++ b/solution.py
@@ -130,13 +130,16 @@
     up_v,
     down_v,
     part_out,
-    part_in,
+    hop_in,
+    hop_sum,
+    pair_in,
     hid,
     proj_out,
     proj_in,
     proj_own,
     fin,
     fin_in,
+    near_y,
     dense,
     w_sem,
     info_send,
@@ -168,7 +171,11 @@
     window = x_own.shape[2]
     shift = held - window
     rest = shift
-    share = part_in.shape[3]
+    share = pair_in.shape[2]
+    lead = window - rest
+    x_peer = base + k + 1 - 2 * (k % 2)
+    z_peer = base + (k + 2) % owners
+    across = owners - 1 - k
 
     loads = [
         pltpu.make_async_copy(src, dst, w_sem.at[i])
@@ -212,6 +219,25 @@
             device_id_type=MESH,
         )
 
+    spans = (pl.ds(0, window), pl.ds(lead, rest))
+
+    def sided(build):
+        return [(t == side, build(spans[side])) for side in range(2)]
+
+    def each(pairs, act):
+        for taken, copy in pairs:
+
+            @pl.when(taken)
+            def _(copy=copy):
+                getattr(copy, act)()
+
+    def from_partner(pairs):
+        for side in range(2):
+
+            @pl.when(other_t == side)
+            def _(copy=pairs[side][1]):
+                copy.wait_recv()
+
     info_copies = [
         remote(
             info,
@@ -226,7 +252,8 @@
         copy.start()
 
     def window_of(block):
-        return tok_ref.at[:, pl.ds((block // 2) * held + (block % 2) * shift, window)]
+        start = (block // 2) * held + (window if block % 2 else 0)
+        return tok_ref.at[:, pl.ds(start, rest if block % 2 else window)]
 
     tok_copies = []
     for block in range(4):
@@ -238,7 +265,7 @@
                 mine,
                 remote(
                     window_of(block),
-                    rows_in.at[k],
+                    rows_in.at[k, :, spans[block % 2]],
                     tok_send.at[block],
                     tok_recv.at[k],
                     {"ep": base + to_k, "tp": to_t},
@@ -252,7 +279,9 @@
 
         @pl.when(mine)
         def _(block=block):
-            pltpu.make_async_copy(window_of(block), rows_in.at[k], tok_recv.at[k]).start()
+            pltpu.make_async_copy(
+                window_of(block), rows_in.at[k, :, spans[block % 2]], tok_recv.at[k]
+            ).start()
 
     info_all[k] = info[...]
     size = owners * tok_rows
@@ -279,92 +308,164 @@
     route[1] = jnp.where(far_place == slots, 1.0, 0.0).astype(jnp.bfloat16)
 
     for j in range(owners):
-        pltpu.make_async_copy(window_of(0), rows_in.at[j], tok_recv.at[j]).wait()
+        for side in range(2):
+
+            @pl.when(t == side)
+            def _(j=j, side=side):
+                pltpu.make_async_copy(
+                    window_of(side), rows_in.at[j, :, spans[side]], tok_recv.at[j]
+                ).wait()
+
     rows = rows_in[...].reshape(size, window)
     x_far_out = x_far.at[2]
     x_far_out[...] = dot(route[1], rows).astype(jnp.bfloat16)
-    far_x = remote(x_far_out, x_far.at[t], xb_sem.at[0], xb_sem.at[1], {"ep": far_ep})
-    far_x.start()
+    far_x = sided(
+        lambda lanes: remote(
+            x_far.at[2, :, lanes],
+            x_far.at[t, :, lanes],
+            xb_sem.at[0],
+            xb_sem.at[1],
+            {"ep": far_ep},
+        )
+    )
+    each(far_x, "start")
     x_own[t] = dot(route[0], rows).astype(jnp.bfloat16)
-    own_x = remote(x_own.at[t], x_own.at[t], xa_sem.at[0], xa_sem.at[1], {"tp": other_t})
-    own_x.start()
-
-    def span(side):
-        return pl.ds(pl.multiple_of(side * shift, 128), window)
+    own_x = sided(
+        lambda lanes: remote(
+            x_own.at[t, :, lanes],
+            x_own.at[t, :, lanes],
+            xa_sem.at[0],
+            xa_sem.at[1],
+            {"tp": other_t},
+        )
+    )
+    each(own_x, "start")
+
+    def span(side, start, count):
+        return pl.ds(pl.multiple_of(side * shift + start, 128), count)
 
     for load in loads[:2]:
         load.wait()
 
-    def spread(half, x_ref, wait_partner):
-        near = span(t)
-        away = pl.ds(pl.multiple_of(other_t * window, 128), rest)
-        lanes = pl.ds(pl.multiple_of(other_t * (window - rest), 128), rest)
-        gate = dot(x_ref[t], gate_v[near])
-        up = dot(x_ref[t], up_v[near])
-        wait_partner()
-        gate = (gate + dot(x_ref[other_t, :, lanes], gate_v[away])).astype(jnp.bfloat16)
-        up = (up + dot(x_ref[other_t, :, lanes], up_v[away])).astype(jnp.bfloat16)
-        for j in range(owners):
-            part_out[half, j, 0] = gate[j * share : (j + 1) * share]
-            part_out[half, j, 1] = up[j * share : (j + 1) * share]
+    def spread(half, x_ref):
+        head, tail = x_ref[0], x_ref[1, :, lead:]
+        for c, w_ref in enumerate((gate_v, up_v)):
+            part = dot(head, w_ref[:window]) + dot(tail, w_ref[window:])
+            part = part.astype(jnp.bfloat16)
+            for j in range(owners):
+                part_out[half, j, c] = part[j * share : (j + 1) * share]
         copies = []
-        for step in range(1, owners):
-            to = (k + step) % owners
+        for slot in range(2):
+            for c, peer in enumerate((x_peer, z_peer)):
+                to = across if slot == 0 else peer - base
+                copies.append(
+                    remote(
+                        part_out.at[half, to, c],
+                        hop_in.at[half, c, slot],
+                        rs_send.at[half, 2 * slot + c],
+                        rs_recv.at[half, 2 * slot + c],
+                        {"ep": peer},
+                    )
+                )
+                copies[-1].start()
+        return copies
+
+    def forward(half, arriving):
+        copies = []
+        for c, peer in enumerate((z_peer, x_peer)):
+            arriving[c].wait_recv()
+            mixed = part_out[half, peer - base, c].astype(jnp.float32)
+            mixed = mixed + hop_in[half, c, 0].astype(jnp.float32)
+            hop_sum[half, c] = mixed.astype(jnp.bfloat16)
             copies.append(
                 remote(
-                    part_out.at[half, to],
-                    part_in.at[half, step - 1],
-                    rs_send.at[half, step - 1],
-                    rs_recv.at[half, step - 1],
-                    {"ep": base + to},
+                    hop_sum.at[half, c],
+                    pair_in.at[half, c],
+                    rs_send.at[half, 4 + c],
+                    rs_recv.at[half, 4 + c],
+                    {"ep": peer},
                 )
             )
             copies[-1].start()
         return copies
 
     def activate(half, arriving):
-        gate = part_out[half, k, 0].astype(jnp.float32)
-        up = part_out[half, k, 1].astype(jnp.float32)
-        for step in range(1, owners):
-            arriving[step - 1].wait_recv()
-            gate = gate + part_in[half, step - 1, 0].astype(jnp.float32)
-            up = up + part_in[half, step - 1, 1].astype(jnp.float32)
-        hid[half, k] = (gate / (1.0 + jnp.exp(-gate)) * up).astype(jnp.bfloat16)
+        for copy in arriving:
+            copy.wait_recv()
+
+        def total(c):
+            out = part_out[half, k, c].astype(jnp.float32)
+            out = out + hop_in[half, c, 1].astype(jnp.float32)
+            return out + pair_in[half, c].astype(jnp.float32)
+
+        gate = total(0)
+        hid[half, k] = (gate / (1.0 + jnp.exp(-gate)) * total(1)).astype(jnp.bfloat16)
         copies = []
-        for step in range(1, owners):
+        for c, peer in enumerate((x_peer, z_peer)):
             copies.append(
                 remote(
                     hid.at[half, k],
                     hid.at[half, k],
-                    ag_send.at[half, step - 1],
-                    ag_recv.at[half, step - 1],
-                    {"ep": base + (k + step) % owners},
+                    ag_send.at[half, c],
+                    ag_recv.at[half, c],
+                    {"ep": peer},
                 )
             )
             copies[-1].start()
         return copies
 
-    def project(half, arriving):
+    def relay(half, arriving):
+        copies = []
+        for c, (source, peer) in enumerate(((x_peer, z_peer), (z_peer, x_peer))):
+            arriving[c].wait_recv()
+            piece = hid.at[half, source - base, pl.ds(c * (share // 2), share // 2)]
+            copies.append(
+                remote(
+                    piece,
+                    piece,
+                    ag_send.at[half, 2 + c],
+                    ag_recv.at[half, 2 + c],
+                    {"ep": peer},
+                )
+            )
+            copies[-1].start()
+        return copies
+
+    def project(half, arriving, chunks):
         for copy in arriving:
             copy.wait_recv()
         hidden = hid[half].reshape(CAP, hid.shape[3])
-        proj_out[half] = dot(hidden, down_v[span(other_t)], ((1,), (1,))).astype(jnp.bfloat16)
-        copy = remote(
-            proj_out.at[half],
-            proj_in.at[half],
-            tp_send.at[half],
-            tp_recv.at[half],
-            {"tp": other_t},
-        )
-        copy.start()
-        proj_own[half] = dot(hidden, down_v[span(t)], ((1,), (1,)))
-        return copy
-
-    def settle(half, copy):
+        copies = []
+        for start, count in chunks:
+            lanes = pl.ds(start, count)
+            proj_out[half, :, lanes] = dot(
+                hidden, down_v[span(other_t, start, count)], ((1,), (1,))
+            ).astype(jnp.bfloat16)
+            copies.append(
+                remote(
+                    proj_out.at[half, :, lanes],
+                    proj_in.at[half, :, lanes],
+                    tp_send.at[half + len(copies)],
+                    tp_recv.at[half + len(copies)],
+                    {"tp": other_t},
+                )
+            )
+            copies[-1].start()
+        for start, count in chunks:
+            proj_own[half, :, pl.ds(start, count)] = dot(
+                hidden, down_v[span(t, start, count)], ((1,), (1,))
+            )
+        return copies
+
+    def settle(half, copy, start, count):
         copy.wait_recv()
-        fin[half] = (proj_own[half] + proj_in[half].astype(jnp.float32)).astype(jnp.bfloat16)
-
-    rs_a = spread(0, x_own, own_x.wait_recv)
+        lanes = pl.ds(start, count)
+        fin[half, :, lanes] = (
+            proj_own[half, :, lanes] + proj_in[half, :, lanes].astype(jnp.float32)
+        ).astype(jnp.bfloat16)
+
+    from_partner(own_x)
+    rs_a = spread(0, x_own)
 
     columns = jnp.transpose(
         jnp.concatenate([near_place, far_place, near_w, far_w, weights[: 8 - 4]], axis=0)
@@ -374,46 +475,72 @@
     scat[0] = jnp.where(columns[:, 0:1] == lanes, 1.0, 0.0).astype(jnp.bfloat16)
     scat[1] = jnp.where(columns[:, 1:2] == lanes, 1.0, 0.0).astype(jnp.bfloat16)
 
-    far_x.wait_recv()
-    pass_x = remote(x_far.at[t], x_far.at[t], xf_sem.at[0], xf_sem.at[1], {"tp": other_t})
-    pass_x.start()
-    rs_b = spread(1, x_far, pass_x.wait_recv)
-    ag_a = activate(0, rs_a)
-    ag_b = activate(1, rs_b)
+    each(far_x, "wait_recv")
+    pass_x = sided(
+        lambda lanes: remote(
+            x_far.at[t, :, lanes],
+            x_far.at[t, :, lanes],
+            xf_sem.at[0],
+            xf_sem.at[1],
+            {"tp": other_t},
+        )
+    )
+    each(pass_x, "start")
+    sum_a = forward(0, rs_a)
+    from_partner(pass_x)
+    rs_b = spread(1, x_far)
+    ag_a = activate(0, rs_a[2:] + sum_a)
+    sum_b = forward(1, rs_b)
+    more_a = relay(0, ag_a)
+    ag_b = activate(1, rs_b[2:] + sum_b)
     loads[2].wait()
-    tp_a = project(0, ag_a)
-    settle(0, tp_a)
-    tp_b = project(1, ag_b)
-    settle(1, tp_b)
-    far_y = remote(fin.at[1], fin_in, far_sem.at[0], far_sem.at[1], {"ep": far_ep})
-    far_y.start()
-    near_y = [
-        row_w[pl.ds(j * tok_rows, tok_rows), 2:3]
-        * dot(scat[0, pl.ds(j * tok_rows, tok_rows)], fin[0])
-        for j in range(owners)
-    ]
-    far_y.wait_recv()
-    to_t = k // 2
-    out_copies = []
-    starts = (0, window)
-    sizes = (window, rest)
+    tp_a = project(0, more_a, [(0, window)])
+    more_b = relay(1, ag_b)
+    settle(0, tp_a[0], 0, window)
+    chunks = [(start, window // 2) for start in (0, window // 2)]
+    tp_b = project(1, more_b, chunks)
+    far_y = []
+    for c, (start, count) in enumerate(chunks):
+        settle(1, tp_b[c], start, count)
+        for side in range(2):
+            begin = max(start, side * lead)
+            lanes = pl.ds(begin, start + count - begin)
+            copy = remote(
+                fin.at[1, :, lanes],
+                fin_in.at[:, lanes],
+                far_sem.at[0, c],
+                far_sem.at[1, c],
+                {"ep": far_ep},
+            )
+            far_y.append((t == side, copy))
+        each(far_y[-2:], "start")
     for j in range(owners):
         rows_j = pl.ds(j * tok_rows, tok_rows)
-        far_part = row_w[rows_j, 3:4] * dot(scat[1, rows_j], fin_in[...])
-        dense[j] = (near_y[j] + far_part).astype(jnp.bfloat16)
-        for side in range(2):
-            from_lanes = pl.ds(window - sizes[side], sizes[side])
-            for part in range(2):
-                picked = jnp.logical_and(t == side, k % 2 == part)
-                mine = jnp.logical_and(k == j, t == to_t)
-                to_lanes = pl.ds(part * held + starts[side], sizes[side])
-                spot = 2 * part + side
-                away = jnp.logical_and(picked, jnp.logical_not(mine))
+        near_y[rows_j] = row_w[rows_j, 2:3] * dot(scat[0, rows_j], fin[0])
+    to_t = k // 2
+    spot = 2 * (k % 2) + t
+    out_copies = []
+    for c, (start, count) in enumerate(chunks):
+        each(far_y[2 * c : 2 * c + 2], "wait_recv")
+        within = pl.ds(start, count)
+        for j in range(owners):
+            rows_j = pl.ds(j * tok_rows, tok_rows)
+            far_part = row_w[rows_j, 3:4] * dot(scat[1, rows_j], fin_in[:, within])
+            dense[j, :, within] = (near_y[rows_j, within] + far_part).astype(jnp.bfloat16)
+            mine = jnp.logical_and(k == j, t == to_t)
+            for side in range(2):
+                begin = max(start, side * lead)
+                size_c = start + count - begin
+                lanes = pl.ds(begin, size_c)
+                to_lanes = pl.ds(
+                    pl.multiple_of((k % 2) * held + side * shift + begin, 128), size_c
+                )
+                away = jnp.logical_and(t == side, jnp.logical_not(mine))
                 copy = remote(
-                    dense.at[j, :, from_lanes],
+                    dense.at[j, :, lanes],
                     out_ref.at[:, to_lanes],
-                    out_send.at[j],
-                    out_recv.at[spot],
+                    out_send.at[j, c],
+                    out_recv.at[spot, c],
                     {"ep": base + j, "tp": to_t},
                 )
                 out_copies.append((away, copy))
@@ -422,10 +549,10 @@
                 def _(copy=copy):
                     copy.start()
 
-                @pl.when(jnp.logical_and(picked, mine))
-                def _(j=j, from_lanes=from_lanes, to_lanes=to_lanes, spot=spot):
+                @pl.when(jnp.logical_and(t == side, mine))
+                def _(j=j, c=c, lanes=lanes, to_lanes=to_lanes):
                     pltpu.make_async_copy(
-                        dense.at[j, :, from_lanes], out_ref.at[:, to_lanes], out_recv.at[spot]
+                        dense.at[j, :, lanes], out_ref.at[:, to_lanes], out_recv.at[spot, c]
                     ).start()
 
     for away, copy in [(jnp.logical_not(mine), copy) for mine, copy in tok_copies] + out_copies:
@@ -434,14 +561,23 @@
         def _(copy=copy):
             copy.wait_send()
 
-    for copy in info_copies + rs_a + rs_b + ag_a + ag_b + [far_x, own_x, pass_x, tp_a, tp_b, far_y]:
+    for pairs in (far_x, own_x, pass_x, far_y):
+        each(pairs, "wait_send")
+    for copy in info_copies + rs_a + rs_b + sum_a + sum_b + ag_a + ag_b + more_a + more_b:
         copy.wait_send()
-    for part in range(2):
-        for side in range(2):
-            here = pl.ds(part * held + starts[side], sizes[side])
-            pltpu.make_async_copy(
-                dense.at[0, :, pl.ds(0, sizes[side])], out_ref.at[:, here], out_recv.at[2 * part + side]
-            ).wait()
+    for copy in tp_a + tp_b:
+        copy.wait_send()
+    for c, (start, count) in enumerate(chunks):
+        for part in range(2):
+            for side in range(2):
+                begin = max(start, side * lead)
+                size_c = start + count - begin
+                here = pl.ds(part * held + side * shift + begin, size_c)
+                pltpu.make_async_copy(
+                    dense.at[0, :, pl.ds(begin, size_c)],
+                    out_ref.at[:, here],
+                    out_recv.at[2 * part + side, c],
+                ).wait()
 
 
 def stay_shards(tokens, expert_ids, gate_values, group_counts, gate_weight, up_weight, down_weight):
@@ -477,13 +613,16 @@
             pltpu.VMEM((held, half_ff), bf16),
             pltpu.VMEM((held, half_ff), bf16),
             pltpu.VMEM((2, owners, 2, share, half_ff), bf16),
-            pltpu.VMEM((2, owners - 1, 2, share, half_ff), bf16),
+            pltpu.VMEM((2, 2, 2, share, half_ff), bf16),
+            pltpu.VMEM((2, 2, share, half_ff), bf16),
+            pltpu.VMEM((2, 2, share, half_ff), bf16),
             pltpu.VMEM((2, owners, share, half_ff), bf16),
             pltpu.VMEM((2, CAP, width), bf16),
             pltpu.VMEM((2, CAP, width), bf16),
             pltpu.VMEM((2, CAP, width), f32),
             pltpu.VMEM((2, CAP, width), bf16),
             pltpu.VMEM((CAP, width), bf16),
+            pltpu.VMEM((size, width), f32),
             pltpu.VMEM((owners, rows, width), bf16),
             dma((3,)),
             dma((owners - 1,)),
@@ -493,15 +632,15 @@
             dma((2,)),
             dma((2,)),
             dma((2,)),
-            dma((2, owners - 1)),
-            dma((2, owners - 1)),
-            dma((2, owners - 1)),
-            dma((2, owners - 1)),
-            dma((2,)),
-            dma((2,)),
-            dma((2,)),
-            dma((owners,)),
-            dma((4,)),
+            dma((2, 6)),
+            dma((2, 6)),
+            dma((2, 4)),
+            dma((2, 4)),
+            dma((3,)),
+            dma((3,)),
+            dma((2, 2)),
+            dma((owners, 2)),
+            dma((4, 2)),
         ],
         compiler_params=pltpu.CompilerParams(collective_id=0, has_side_effects=True),
     )(group_counts, expert_ids.T, gate_values.T, tokens, gate_weight, up_weight, down_weight)

time: 57.5 us -> 54.4 us (0.946)
  Pallas kernels: 55.5 us -> 52.4 us
    pallas_call x1, Pallas kernels: 55.5 us -> 52.4 us  [stay_shards(): pl.pallas_call(functools.partial(owner_kernel, owners), out_shape=jax.Sha...]
where the time goes in v3:
time: 54.4 us; the launch traced here: 54.2 us
  Pallas kernels  52.4 us (96%)
  local copies, waits for them, and re-layouts  1.82 us (3%)
    pallas_call x1, Pallas kernels, stay_shards(): pl.pallas_call(functools.partial(owner_kernel, owners), out_shape=jax.Sha...  52.4 us
    unnamed x1, local copies, waits for them, and re-layouts  1.82 us

profile of v3, /device:TPU:0, one launch (start us, length us, event | category | flops | bytes accessed | tf_op | source)
XLA Modules:
  0.0 54.2 jit_solution(4834977137879565414)
XLA Ops:
  0.0 52.4 %shard_map.73 = bf16[128,1792]{1,0:T(8,128)(2,1)} custom-call(s32[2]{0:T(128)} %count_ref.1, s32[8,128]{1,0:T(8,128)} %bitcast.2, f32[8,128]{1,0:T(8,128)} %bitcast.3, bf16[128,1792]{1,0:T(8,128)(2,1)} %tok_ref.1, bf16[896,1280]{1,0:T(8,128)(2,1)} %gate_ref.1, bf16[896,1280]{1,0:T(8,128)(2,1)} %up_ref.1, bf16[896,1280]{1,0:T(8,128)(2,1)} %down_ref.1), custom_call_target="tpu_custom_call" | custom-call | tf_op jit(solution)/shard_map/pallas_call | solution.py:593
  52.4 1.8 %copy.9 = bf16[128,1792]{1,0:T(8,128)(2,1)} copy(bf16[128,1792]{1,0:T(8,128)(2,1)} %shard_map.73) | data formatting | bytes 917504

commit v4 on v3

--- a/solution.py
+++ b/solution.py
@@ -219,10 +219,14 @@
             device_id_type=MESH,
         )
 
-    spans = (pl.ds(0, window), pl.ds(lead, rest))
-
-    def sided(build):
-        return [(t == side, build(spans[side])) for side in range(2)]
+    halves = [(0, window // 2), (window // 2, window // 2)]
+
+    def cut_at(side, start, count):
+        begin = max(start, side * lead)
+        return begin, start + count - begin
+
+    def sided(build, start, count):
+        return [(t == side, build(pl.ds(*cut_at(side, start, count)))) for side in range(2)]
 
     def each(pairs, act):
         for taken, copy in pairs:
@@ -251,37 +255,35 @@
     for copy in info_copies:
         copy.start()
 
-    def window_of(block):
-        start = (block // 2) * held + (window if block % 2 else 0)
-        return tok_ref.at[:, pl.ds(start, rest if block % 2 else window)]
+    def window_of(block, begin, count):
+        start = (block // 2) * held + (block % 2) * shift + begin
+        return tok_ref.at[:, pl.ds(start, count)]
 
     tok_copies = []
-    for block in range(4):
-        to_k = 2 * t + block // 2
-        to_t = block % 2
-        mine = jnp.logical_and(k == to_k, t == to_t)
-        tok_copies.append(
-            (
-                mine,
-                remote(
-                    window_of(block),
-                    rows_in.at[k, :, spans[block % 2]],
-                    tok_send.at[block],
-                    tok_recv.at[k],
-                    {"ep": base + to_k, "tp": to_t},
-                ),
-            )
-        )
-
-        @pl.when(jnp.logical_not(mine))
-        def _(copy=tok_copies[-1][1]):
-            copy.start()
-
-        @pl.when(mine)
-        def _(block=block):
-            pltpu.make_async_copy(
-                window_of(block), rows_in.at[k, :, spans[block % 2]], tok_recv.at[k]
-            ).start()
+    for c, half_span in enumerate(halves):
+        for block in range(4):
+            to_k = 2 * t + block // 2
+            to_t = block % 2
+            mine = jnp.logical_and(k == to_k, t == to_t)
+            begin, count = cut_at(to_t, *half_span)
+            source = window_of(block, begin, count)
+            target = rows_in.at[k, :, pl.ds(begin, count)]
+            copy = remote(
+                source,
+                target,
+                tok_send.at[block, c],
+                tok_recv.at[k, c],
+                {"ep": base + to_k, "tp": to_t},
+            )
+            tok_copies.append((mine, copy))
+
+            @pl.when(jnp.logical_not(mine))
+            def _(copy=copy):
+                copy.start()
+
+            @pl.when(mine)
+            def _(source=source, target=target, c=c):
+                pltpu.make_async_copy(source, target, tok_recv.at[k, c]).start()
 
     info_all[k] = info[...]
     size = owners * tok_rows
@@ -307,39 +309,47 @@
     route[0] = jnp.where(near_place == slots, 1.0, 0.0).astype(jnp.bfloat16)
     route[1] = jnp.where(far_place == slots, 1.0, 0.0).astype(jnp.bfloat16)
 
-    for j in range(owners):
-        for side in range(2):
-
-            @pl.when(t == side)
-            def _(j=j, side=side):
-                pltpu.make_async_copy(
-                    window_of(side), rows_in.at[j, :, spans[side]], tok_recv.at[j]
-                ).wait()
-
-    rows = rows_in[...].reshape(size, window)
-    x_far_out = x_far.at[2]
-    x_far_out[...] = dot(route[1], rows).astype(jnp.bfloat16)
-    far_x = sided(
-        lambda lanes: remote(
-            x_far.at[2, :, lanes],
-            x_far.at[t, :, lanes],
-            xb_sem.at[0],
-            xb_sem.at[1],
-            {"ep": far_ep},
-        )
-    )
-    each(far_x, "start")
-    x_own[t] = dot(route[0], rows).astype(jnp.bfloat16)
-    own_x = sided(
-        lambda lanes: remote(
-            x_own.at[t, :, lanes],
-            x_own.at[t, :, lanes],
-            xa_sem.at[0],
-            xa_sem.at[1],
-            {"tp": other_t},
-        )
-    )
-    each(own_x, "start")
+    far_x, own_x = [], []
+    for c, half_span in enumerate(halves):
+        for j in range(owners):
+            for side in range(2):
+
+                @pl.when(t == side)
+                def _(j=j, side=side, c=c, piece=cut_at(side, *half_span)):
+                    pltpu.make_async_copy(
+                        window_of(side, *piece), rows_in.at[j, :, pl.ds(*piece)], tok_recv.at[j, c]
+                    ).wait()
+
+        within = pl.ds(*half_span)
+        rows = rows_in[:, :, within].reshape(size, half_span[1])
+        x_far[2, :, within] = dot(route[1], rows).astype(jnp.bfloat16)
+        far_x.append(
+            sided(
+                lambda lanes: remote(
+                    x_far.at[2, :, lanes],
+                    x_far.at[t, :, lanes],
+                    xb_sem.at[0, c],
+                    xb_sem.at[1, c],
+                    {"ep": far_ep},
+                ),
+                *half_span,
+            )
+        )
+        each(far_x[-1], "start")
+        x_own[t, :, within] = dot(route[0], rows).astype(jnp.bfloat16)
+        own_x.append(
+            sided(
+                lambda lanes: remote(
+                    x_own.at[t, :, lanes],
+                    x_own.at[t, :, lanes],
+                    xa_sem.at[0, c],
+                    xa_sem.at[1, c],
+                    {"tp": other_t},
+                ),
+                *half_span,
+            )
+        )
+        each(own_x[-1], "start")
 
     def span(side, start, count):
         return pl.ds(pl.multiple_of(side * shift + start, 128), count)
@@ -464,7 +474,8 @@
             proj_own[half, :, lanes] + proj_in[half, :, lanes].astype(jnp.float32)
         ).astype(jnp.bfloat16)
 
-    from_partner(own_x)
+    for pairs in own_x:
+        from_partner(pairs)
     rs_a = spread(0, x_own)
 
     columns = jnp.transpose(
@@ -475,19 +486,25 @@
     scat[0] = jnp.where(columns[:, 0:1] == lanes, 1.0, 0.0).astype(jnp.bfloat16)
     scat[1] = jnp.where(columns[:, 1:2] == lanes, 1.0, 0.0).astype(jnp.bfloat16)
 
-    each(far_x, "wait_recv")
-    pass_x = sided(
-        lambda lanes: remote(
-            x_far.at[t, :, lanes],
-            x_far.at[t, :, lanes],
-            xf_sem.at[0],
-            xf_sem.at[1],
-            {"tp": other_t},
-        )
-    )
-    each(pass_x, "start")
+    pass_x = []
+    for c, half_span in enumerate(halves):
+        each(far_x[c], "wait_recv")
+        pass_x.append(
+            sided(
+                lambda lanes: remote(
+                    x_far.at[t, :, lanes],
+                    x_far.at[t, :, lanes],
+                    xf_sem.at[0, c],
+                    xf_sem.at[1, c],
+                    {"tp": other_t},
+                ),
+                *half_span,
+            )
+        )
+        each(pass_x[-1], "start")
     sum_a = forward(0, rs_a)
-    from_partner(pass_x)
+    for pairs in pass_x:
+        from_partner(pairs)
     rs_b = spread(1, x_far)
     ag_a = activate(0, rs_a[2:] + sum_a)
     sum_b = forward(1, rs_b)
@@ -497,23 +514,27 @@
     tp_a = project(0, more_a, [(0, window)])
     more_b = relay(1, ag_b)
     settle(0, tp_a[0], 0, window)
-    chunks = [(start, window // 2) for start in (0, window // 2)]
-    tp_b = project(1, more_b, chunks)
+    tp_b = project(1, more_b, halves)
+    small = window // 4
+    chunks = [halves[0], (2 * small, small), (3 * small, small)]
     far_y = []
     for c, (start, count) in enumerate(chunks):
-        settle(1, tp_b[c], start, count)
-        for side in range(2):
-            begin = max(start, side * lead)
-            lanes = pl.ds(begin, start + count - begin)
-            copy = remote(
-                fin.at[1, :, lanes],
-                fin_in.at[:, lanes],
-                far_sem.at[0, c],
-                far_sem.at[1, c],
-                {"ep": far_ep},
-            )
-            far_y.append((t == side, copy))
-        each(far_y[-2:], "start")
+        if c < 2:
+            settle(1, tp_b[c], *halves[c])
+        far_y.append(
+            sided(
+                lambda lanes: remote(
+                    fin.at[1, :, lanes],
+                    fin_in.at[:, lanes],
+                    far_sem.at[0, c],
+                    far_sem.at[1, c],
+                    {"ep": far_ep},
+                ),
+                start,
+                count,
+            )
+        )
+        each(far_y[-1], "start")
     for j in range(owners):
         rows_j = pl.ds(j * tok_rows, tok_rows)
         near_y[rows_j] = row_w[rows_j, 2:3] * dot(scat[0, rows_j], fin[0])
@@ -521,7 +542,7 @@
     spot = 2 * (k % 2) + t
     out_copies = []
     for c, (start, count) in enumerate(chunks):
-        each(far_y[2 * c : 2 * c + 2], "wait_recv")
+        each(far_y[c], "wait_recv")
         within = pl.ds(start, count)
         for j in range(owners):
             rows_j = pl.ds(j * tok_rows, tok_rows)
@@ -529,8 +550,7 @@
             dense[j, :, within] = (near_y[rows_j, within] + far_part).astype(jnp.bfloat16)
             mine = jnp.logical_and(k == j, t == to_t)
             for side in range(2):
-                begin = max(start, side * lead)
-                size_c = start + count - begin
+                begin, size_c = cut_at(side, start, count)
                 lanes = pl.ds(begin, size_c)
                 to_lanes = pl.ds(
                     pl.multiple_of((k % 2) * held + side * shift + begin, 128), size_c
@@ -561,7 +581,7 @@
         def _(copy=copy):
             copy.wait_send()
 
-    for pairs in (far_x, own_x, pass_x, far_y):
+    for pairs in far_x + own_x + pass_x + far_y:
         each(pairs, "wait_send")
     for copy in info_copies + rs_a + rs_b + sum_a + sum_b + ag_a + ag_b + more_a + more_b:
         copy.wait_send()
@@ -570,8 +590,7 @@
     for c, (start, count) in enumerate(chunks):
         for part in range(2):
             for side in range(2):
-                begin = max(start, side * lead)
-                size_c = start + count - begin
+                begin, size_c = cut_at(side, start, count)
                 here = pl.ds(part * held + side * shift + begin, size_c)
                 pltpu.make_async_copy(
                     dense.at[0, :, pl.ds(begin, size_c)],
@@ -627,20 +646,20 @@
             dma((3,)),
             dma((owners - 1,)),
             dma((owners - 1,)),
-            dma((4,)),
-            dma((owners,)),
-            dma((2,)),
-            dma((2,)),
-            dma((2,)),
+            dma((4, 2)),
+            dma((owners, 2)),
+            dma((2, 2)),
+            dma((2, 2)),
+            dma((2, 2)),
             dma((2, 6)),
             dma((2, 6)),
             dma((2, 4)),
             dma((2, 4)),
             dma((3,)),
             dma((3,)),
-            dma((2, 2)),
-            dma((owners, 2)),
-            dma((4, 2)),
+            dma((2, 3)),
+            dma((owners, 3)),
+            dma((4, 3)),
         ],
         compiler_params=pltpu.CompilerParams(collective_id=0, has_side_effects=True),
     )(group_counts, expert_ids.T, gate_values.T, tokens, gate_weight, up_weight, down_weight)

time: 54.4 us -> 54.4 us (level)
  no operation moved by 1% of the time
where the time goes in v4:
time: 54.4 us; the launch traced here: 54.2 us
  Pallas kernels  52.4 us (96%)
  local copies, waits for them, and re-layouts  1.82 us (3%)
    pallas_call x1, Pallas kernels, stay_shards(): pl.pallas_call(functools.partial(owner_kernel, owners), out_shape=jax.Sha...  52.4 us
    unnamed x1, local copies, waits for them, and re-layouts  1.82 us

profile of v4, /device:TPU:0, one launch (start us, length us, event | category | flops | bytes accessed | tf_op | source)
XLA Modules:
  0.0 54.2 jit_solution(6232947186056183006)
XLA Ops:
  0.0 52.4 %shard_map.73 = bf16[128,1792]{1,0:T(8,128)(2,1)} custom-call(s32[2]{0:T(128)} %count_ref.1, s32[8,128]{1,0:T(8,128)} %bitcast.2, f32[8,128]{1,0:T(8,128)} %bitcast.3, bf16[128,1792]{1,0:T(8,128)(2,1)} %tok_ref.1, bf16[896,1280]{1,0:T(8,128)(2,1)} %gate_ref.1, bf16[896,1280]{1,0:T(8,128)(2,1)} %up_ref.1, bf16[896,1280]{1,0:T(8,128)(2,1)} %down_ref.1), custom_call_target="tpu_custom_call" | custom-call | tf_op jit(solution)/shard_map/pallas_call | solution.py:612
  52.4 1.8 %copy.9 = bf16[128,1792]{1,0:T(8,128)(2,1)} copy(bf16[128,1792]{1,0:T(8,128)(2,1)} %shard_map.73) | data formatting | bytes 917504

commit v5 on v4

--- a/solution.py
+++ b/solution.py
@@ -411,30 +411,13 @@
         gate = total(0)
         hid[half, k] = (gate / (1.0 + jnp.exp(-gate)) * total(1)).astype(jnp.bfloat16)
         copies = []
-        for c, peer in enumerate((x_peer, z_peer)):
+        for c, peer in enumerate((base + across, x_peer, z_peer)):
             copies.append(
                 remote(
                     hid.at[half, k],
                     hid.at[half, k],
                     ag_send.at[half, c],
                     ag_recv.at[half, c],
-                    {"ep": peer},
-                )
-            )
-            copies[-1].start()
-        return copies
-
-    def relay(half, arriving):
-        copies = []
-        for c, (source, peer) in enumerate(((x_peer, z_peer), (z_peer, x_peer))):
-            arriving[c].wait_recv()
-            piece = hid.at[half, source - base, pl.ds(c * (share // 2), share // 2)]
-            copies.append(
-                remote(
-                    piece,
-                    piece,
-                    ag_send.at[half, 2 + c],
-                    ag_recv.at[half, 2 + c],
                     {"ep": peer},
                 )
             )
@@ -508,13 +491,11 @@
     rs_b = spread(1, x_far)
     ag_a = activate(0, rs_a[2:] + sum_a)
     sum_b = forward(1, rs_b)
-    more_a = relay(0, ag_a)
     ag_b = activate(1, rs_b[2:] + sum_b)
     loads[2].wait()
-    tp_a = project(0, more_a, [(0, window)])
-    more_b = relay(1, ag_b)
+    tp_a = project(0, ag_a, [(0, window)])
     settle(0, tp_a[0], 0, window)
-    tp_b = project(1, more_b, halves)
+    tp_b = project(1, ag_b, halves)
     small = window // 4
     chunks = [halves[0], (2 * small, small), (3 * small, small)]
     far_y = []
@@ -583,7 +564,7 @@
 
     for pairs in far_x + own_x + pass_x + far_y:
         each(pairs, "wait_send")
-    for copy in info_copies + rs_a + rs_b + sum_a + sum_b + ag_a + ag_b + more_a + more_b:
+    for copy in info_copies + rs_a + rs_b + sum_a + sum_b + ag_a + ag_b:
         copy.wait_send()
     for copy in tp_a + tp_b:
         copy.wait_send()

time: 54.4 us -> 53.2 us (0.978)
  Pallas kernels: 52.4 us -> 51.2 us
    pallas_call x1, Pallas kernels: 52.4 us -> 51.2 us  [stay_shards(): pl.pallas_call(functools.partial(owner_kernel, owners), out_shape=jax.Sha...]
where the time goes in v5:
time: 53.2 us; the launch traced here: 53 us
  Pallas kernels  51.2 us (96%)
  local copies, waits for them, and re-layouts  1.82 us (3%)
    pallas_call x1, Pallas kernels, stay_shards(): pl.pallas_call(functools.partial(owner_kernel, owners), out_shape=jax.Sha...  51.2 us
    unnamed x1, local copies, waits for them, and re-layouts  1.82 us

profile of v5, /device:TPU:0, one launch (start us, length us, event | category | flops | bytes accessed | tf_op | source)
XLA Modules:
  0.0 53.0 jit_solution(7909998047721036397)
XLA Ops:
  0.0 51.2 %shard_map.73 = bf16[128,1792]{1,0:T(8,128)(2,1)} custom-call(s32[2]{0:T(128)} %count_ref.1, s32[8,128]{1,0:T(8,128)} %bitcast.2, f32[8,128]{1,0:T(8,128)} %bitcast.3, bf16[128,1792]{1,0:T(8,128)(2,1)} %tok_ref.1, bf16[896,1280]{1,0:T(8,128)(2,1)} %gate_ref.1, bf16[896,1280]{1,0:T(8,128)(2,1)} %up_ref.1, bf16[896,1280]{1,0:T(8,128)(2,1)} %down_ref.1), custom_call_target="tpu_custom_call" | custom-call | tf_op jit(solution)/shard_map/pallas_call | solution.py:593
  51.2 1.8 %copy.9 = bf16[128,1792]{1,0:T(8,128)(2,1)} copy(bf16[128,1792]{1,0:T(8,128)(2,1)} %shard_map.73) | data formatting | bytes 917504
